TPU v7x, 32 devices: a whole 2x2x4 slice. The times are simulated.
32 devices in a mesh: groups: 2 (over y), ctx: 4 (over z), exp: 2 (over x), tp: 2 (over core).
Axes of the slice: x: 2, y: 2, z: 4, core: 2. Of those that a mesh axis runs over, the one named last changes fastest.
Arguments:
- queries: bfloat16 [4, 512, 20, 128], P(('groups', 'exp'), 'ctx', 'tp'), parts along dimension 0, may hold values from -9 to 9
- key_states: bfloat16 [4, 512, 4, 128], P(('groups', 'exp'), 'ctx', 'tp'), parts along dimension 0, may hold values from -9 to 9
- values: bfloat16 [4, 512, 4, 128], P(('groups', 'exp'), 'ctx', 'tp'), parts along dimension 0, may hold values from -6 to 6
- doc_ids: int32 [4, 512], P(('groups', 'exp'), 'ctx'), parts along dimension 0, may hold values from 0 to 3, never falling along the last dimension, each value on 1 to 256 neighbouring positions
- residual: bfloat16 [4, 512, 5120], P(('groups', 'exp'), ('ctx', 'tp')), parts along dimension 0, may hold values from -6 to 6
- out_proj: bfloat16 [2560, 5120], P('tp', 'ctx'), may hold values from -0.125 to 0.125
- norm_gain: bfloat16 [5120], replicated, may hold values from 0.5 to 1.5
- router: bfloat16 [5120, 64], P(None, 'exp'), may hold values from -0.078125 to 0.078125
- expert_ids: int32 [4, 512, 1], P(('groups', 'exp'), ('ctx', 'tp')), parts along dimension 0, may hold values from 0 to 63; in each aligned block of 64 rows (0 to 63, 64 to 127, ..., all dimensions but the last counted through in order) at most 2 rows name the same one
- keep_counts: int32 [128], P('groups'), parts along dimension 0, may hold values from 1 to 2
Outputs:
- expert_inputs: bfloat16 [32, 64, 2, 5120], P(('groups', 'ctx', 'tp'), 'exp'), parts along dimension 0
There are 2 independent parts, one for each index of `groups`. A program takes and returns all parts, laid end to end along the dimension named above; an argument that names none is the same for every part. Nothing has to cross between parts.
Inputs may be any that keep to these rules, and one draw needn't show every extreme that they name: `doc_ids`: doc ids never fall along a request; a document holds at most 256 tokens, and some document holds exactly that many. `expert_ids`: in each aligned block of 64 tokens (the rows of one device) no expert is named more than 2 times, and in some blocks one expert is named exactly 2 times.
All inputs are finite; a program needn't handle non-finite values.
Results may differ from a plain program's by a relative error of at most 0.013.
Values may be sent and summed in bfloat16 or wider, within the bound.
A program may use at most 64 MiB of HBM per device.

v0:
```python
import math

import jax
import jax.numpy as jnp
from jax import lax
from jax.sharding import PartitionSpec as P

CAP = 2


EPSILON = 1e-05


def on_device(
    queries,
    key_states,
    values,
    doc_ids,
    residual,
    out_proj,
    norm_gain,
    router,
    expert_ids,
    keep_counts,
):
    tokens_here = queries.shape[1]
    heads_here = queries.shape[2]
    head_size = queries.shape[3]
    groups_here = key_states.shape[2]
    mixing_ratio = heads_here // groups_here
    ctx_count = lax.axis_size("ctx")
    pair_count = lax.axis_size("tp")
    part_rows = tokens_here // pair_count
    first_token = lax.axis_index("ctx") * tokens_here
    scale = 1.0 / math.sqrt(head_size)
    query_rows = (
        queries[0].reshape(tokens_here, groups_here, mixing_ratio, head_size).transpose(1, 0, 2, 3)
    )
    query_rows = query_rows.reshape(groups_here, tokens_here * mixing_ratio, head_size)
    query_place = (
        first_token
        + lax.broadcasted_iota(jnp.int32, (tokens_here * mixing_ratio,), 0) // mixing_ratio
    )
    query_docs = jnp.repeat(doc_ids[0], mixing_ratio)

    def update(running, key_block, value_block, doc_block, key_first):
        highest, totals, accum = running
        scores = (
            jnp.einsum("gqd,kgd->gqk", query_rows, key_block, preferred_element_type=jnp.float32)
            * scale
        )
        key_place = key_first + lax.broadcasted_iota(jnp.int32, (key_block.shape[0],), 0)
        allowed = (key_place[None, :] <= query_place[:, None]) & (
            doc_block[None, :] == query_docs[:, None]
        )
        masked = jnp.where(allowed[None], scores, -1e30)
        new_highest = jnp.maximum(highest, jnp.max(masked, axis=2))
        weights = jnp.where(allowed[None], jnp.exp(scores - new_highest[..., None]), 0.0)
        factor = jnp.exp(highest - new_highest)
        totals = totals * factor + jnp.sum(weights, axis=2)
        accum = accum * factor[..., None] + jnp.einsum(
            "gqk,kgd->gqd",
            weights.astype(jnp.bfloat16),
            value_block,
            preferred_element_type=jnp.float32,
        )
        return (new_highest, totals, accum)

    start_state = (
        jnp.full((groups_here, tokens_here * mixing_ratio), -1e30, jnp.float32),
        jnp.zeros((groups_here, tokens_here * mixing_ratio), jnp.float32),
        jnp.zeros((groups_here, tokens_here * mixing_ratio, head_size), jnp.float32),
    )
    key_piece = lax.all_gather(key_states, "ctx", axis=1, tiled=True)
    value_piece = lax.all_gather(values, "ctx", axis=1, tiled=True)
    doc_piece = lax.all_gather(doc_ids, "ctx", axis=1, tiled=True)
    piece_rows = key_piece.shape[1]
    block_rows = math.gcd(piece_rows, 512)

    def step(block_number, inner):
        block_offset = block_number * block_rows
        key_block = lax.dynamic_slice_in_dim(key_piece[0], block_offset, block_rows, 0)
        value_block = lax.dynamic_slice_in_dim(value_piece[0], block_offset, block_rows, 0)
        doc_block = lax.dynamic_slice_in_dim(doc_piece[0], block_offset, block_rows, 0)
        return update(inner, key_block, value_block, doc_block, block_offset)

    highest, totals, accum = lax.fori_loop(0, piece_rows // block_rows, step, start_state)
    blended_output = (accum / totals[..., None]).astype(jnp.bfloat16)
    blended_output = blended_output.reshape(
        groups_here, tokens_here, mixing_ratio, head_size
    ).transpose(1, 0, 2, 3)
    attn_rows = blended_output.reshape(pair_count, part_rows, heads_here * head_size)
    columns = out_proj.shape[1]
    gathered = lax.all_gather(attn_rows, "ctx", axis=1, tiled=True)
    gathered = gathered.reshape(pair_count * ctx_count * part_rows, heads_here * head_size)
    own_columns = lax.psum_scatter(
        jnp.dot(gathered, out_proj, preferred_element_type=jnp.float32).astype(jnp.bfloat16),
        "tp",
        scatter_dimension=0,
        tiled=True,
    ).astype(jnp.float32)
    own_columns = own_columns.reshape(ctx_count, part_rows, columns)
    projected = (
        lax.all_to_all(
            own_columns.astype(jnp.bfloat16), "ctx", split_axis=0, concat_axis=2, tiled=True
        )
        .astype(own_columns.dtype)
        .reshape(part_rows, columns * ctx_count)
    )
    hidden = residual[0].astype(jnp.float32) + projected
    power = jnp.mean(hidden * hidden, axis=1, keepdims=True)
    normed = (hidden * lax.rsqrt(power + EPSILON) * norm_gain.astype(jnp.float32)).astype(
        jnp.bfloat16
    )
    expert_count = keep_counts.shape[0]
    chosen = expert_ids[0, :, 0]
    onehot = (
        chosen[:, None] == lax.broadcasted_iota(jnp.int32, (part_rows, expert_count), 1)
    ).astype(jnp.float32)
    lower = (
        lax.broadcasted_iota(jnp.int32, (part_rows, part_rows), 0)
        > lax.broadcasted_iota(jnp.int32, (part_rows, part_rows), 1)
    ).astype(jnp.float32)
    earlier = jnp.dot(lower, onehot, preferred_element_type=jnp.float32)
    ranking = jnp.sum(onehot * earlier, axis=1)
    limits = jnp.sum(onehot * keep_counts.astype(jnp.float32)[None, :], axis=1)
    kept = ranking < limits
    target = chosen.astype(jnp.float32) * CAP + ranking
    slot_iota = lax.broadcasted_iota(jnp.int32, (expert_count * CAP, part_rows), 0).astype(
        jnp.float32
    )
    table = (slot_iota == target[None, :]) & kept[None, :]
    outgoing = jnp.dot(
        table.astype(jnp.bfloat16), normed, preferred_element_type=jnp.float32
    ).astype(jnp.bfloat16)
    exp_count = lax.axis_size("exp")
    outgoing = outgoing.reshape(exp_count, expert_count // exp_count, CAP, normed.shape[1])
    arrived = lax.all_to_all(outgoing, "exp", split_axis=0, concat_axis=0, tiled=True)
    logits = jnp.einsum("secd,de->sec", arrived, router, preferred_element_type=jnp.float32)
    return (arrived.astype(jnp.float32) * jax.nn.sigmoid(logits)[..., None]).astype(jnp.bfloat16)


def solution(mesh):
    placed = (
        P(("groups", "exp"), "ctx", "tp", None),
        P(("groups", "exp"), "ctx", "tp", None),
        P(("groups", "exp"), "ctx", "tp", None),
        P(("groups", "exp"), "ctx"),
        P(("groups", "exp"), ("ctx", "tp"), None),
        P("tp", "ctx"),
        P(),
        P(None, "exp"),
        P(("groups", "exp"), ("ctx", "tp"), None),
        P("groups"),
    )
    return jax.shard_map(
        on_device,
        mesh=mesh,
        in_specs=placed,
        out_specs=P(("groups", "ctx", "tp"), "exp", None, None),
        check_vma=False,
    )
```

profile of v0, /device:TPU:0, one launch (start us, length us, event | category | flops | bytes accessed | tf_op | source)
XLA Modules:
  0.0 172.3 jit_solution(3476322581073212627)
XLA Ops:
  6.5 0.0 copy-start
  6.5 0.0 all-gather.2.cloned.1.call-start
  6.5 12.9 %all_gather.14 = s32[1,512]{1,0:T(1,128)S(1)} all-gather(s32[1,128]{1,0:T(1,128)} %param.13), channel_id=1, replica_groups=mesh['groups'=2,'ctx'=4,'exp'=2,'tp'=2] {'ctx'}, dimensions={1}, use_global_device_ids=true | all-gather | bytes 2560 | tf_op jit(solution)/shard_map/all_gather | solution.py:76
  19.5 0.7 broadcast_in_dim.55
  20.2 0.2 eq.47
  20.4 0.9 copy.17
  21.3 13.9 %all_gather.16 = bf16[1,512,2,128]{3,1,2,0:T(8,128)(2,1)S(1)} all-gather(bf16[1,128,2,128]{3,1,2,0:T(8,128)(2,1)S(1)} %copy.17), channel_id=1, replica_groups=mesh['groups'=2,'ctx'=4,'exp'=2,'tp'=2] {'ctx'}, dimensions={1}, use_global_device_ids=true | all-gather | bytes 327680 | tf_op jit(solution)/shard_map/all_gather | solution.py:74
  35.2 1.3 copy.16
  36.5 0.3 fusion.7
  36.8 0.7 select_reduce_fusion
  37.5 0.0 copy-start.2
  37.5 0.6 fusion
  38.1 0.2 copy-done.2
  38.3 14.1 %all_gather.17 = bf16[1,512,2,128]{3,1,2,0:T(8,128)(2,1)S(1)} all-gather(bf16[1,128,2,128]{3,1,2,0:T(8,128)(2,1)S(1)} %copy.19), channel_id=1, replica_groups=mesh['groups'=2,'ctx'=4,'exp'=2,'tp'=2] {'ctx'}, dimensions={1}, use_global_device_ids=true | all-gather | bytes 327680 | tf_op jit(solution)/shard_map/all_gather | solution.py:75
  52.5 1.2 fusion.18
  53.7 0.3 copy.21
  54.0 0.9 copy.22
  54.9 2.2 %reshape.135 = bf16[2,64,1280]{2,1,0:T(8,128)(2,1)} reshape(bf16[128,2,5,128]{3,2,1,0:T(8,128)(2,1)} %copy.22) | data formatting | bytes 655360 | tf_op jit(solution)/shard_map/reshape | solution.py:92
  57.1 0.0 all-gather.2.cloned.1.call-update
  57.1 0.0 reduce-scatter.2.cloned.1.call-start
  57.1 30.9 %all-gather.2.cloned.1.call-done = bf16[2,256,1280]{2,1,0:T(8,128)(2,1)} async-done(((bf16[2,64,1280]{2,1,0:T(8,128)(2,1)}), bf16[2,256,1280]{2,1,0:T(8,128)(2,1)}) %all-gather.2.cloned.1.call-update) | async-done | bytes 1310736 | tf_op jit(solution)/shard_map/all_gather | solution.py:94
  88.1 0.0 copy-done
  88.1 4.2 %convolution_convert_fusion.1 = bf16[512,1280]{1,0:T(8,128)(2,1)} fusion(bf16[512,1280]{1,0:T(8,128)(2,1)} %bitcast.62, bf16[1280,1280]{1,0:T(8,128)(2,1)S(1)} %copy-done), kind=kOutput, calls=%fused_computation.1 | convolution fusion | flops 1678376960 | bytes 5898240 | tf_op jit(solution)/shard_map/dot_general | solution.py:97
  92.3 0.0 copy-start.6
  92.3 0.0 copy-start.3
  92.3 0.0 copy-start.4
  92.3 0.0 reduce-scatter.2.cloned.1.call-update
  92.3 7.9 %reduce-scatter.2.cloned.1.call-done = bf16[256,1280]{1,0:T(8,128)(2,1)} async-done(((bf16[512,1280]{1,0:T(8,128)(2,1)}), bf16[256,1280]{1,0:T(8,128)(2,1)}) %reduce-scatter.2.cloned.1.call-update) | async-done | bytes 655376 | tf_op jit(solution)/shard_map/reduce_scatter | solution.py:96
  100.3 5.0 %all-to-all-start = ((bf16[4,64,1280]{2,1,0:T(8,128)(2,1)}), bf16[4,64,1280]{2,1,0:T(8,128)(2,1)}, u32[]{:S(2)}, u32[]{:S(2)}) async-start(bf16[4,64,1280]{2,1,0:T(8,128)(2,1)} %bitcast.55), calls=%async_computation.1 | async-start | bytes 1310720 | tf_op jit(solution)/shard_map/all_to_all | solution.py:104
  105.3 0.0 copy-done.6
  105.3 0.0 copy-done.3
  105.3 0.0 copy-done.4
  105.3 0.2 fusion.14
  105.4 0.1 select_reduce_fusion.1
  105.6 17.4 %all-to-all-done = bf16[4,64,1280]{2,1,0:T(8,128)(2,1)} async-done(((bf16[4,64,1280]{2,1,0:T(8,128)(2,1)}), bf16[4,64,1280]{2,1,0:T(8,128)(2,1)}, u32[]{:S(2)}, u32[]{:S(2)}) %all-to-all-start) | async-done | bytes 655392 | tf_op jit(solution)/shard_map/all_to_all | solution.py:104
  123.0 1.2 convert_bitcast_fusion
  124.2 0.8 copy.23
  125.0 0.0 copy-start.1
  125.0 0.2 copy.28
  125.3 0.8 copy-done.1
  126.1 0.3 multiply_reduce_fusion
  126.4 1.6 convolution_convert_fusion
  128.0 3.9 %reshape.137 = bf16[2,32,2,5120]{3,2,1,0:T(2,128)(2,1)} reshape(bf16[128,5120]{1,0:T(8,128)(2,1)} %convolution_convert_fusion) | data formatting | bytes 2621440 | tf_op jit(solution)/shard_map/reshape | solution.py:137
  131.9 0.0 copy-start.5
  131.9 19.7 %all_to_all.14 = bf16[2,32,2,5120]{3,2,1,0:T(2,128)(2,1)S(1)} all-to-all(bf16[2,32,2,5120]{3,2,1,0:T(2,128)(2,1)} %reshape.137), channel_id=1, replica_groups=mesh['groups'=2,'ctx'=4,'exp'=2,'tp'=2] {'exp'}, dimensions={0} | all-to-all | bytes 2621440 | tf_op jit(solution)/shard_map/all_to_all | solution.py:138
  151.6 0.0 copy-done.5
  151.6 11.5 %fusion.9 = f32[32,1,2,2]{3,1,2,0:T(1,128)S(1)} fusion(bf16[2,32,2,5120]{3,2,1,0:T(2,128)(2,1)S(1)} %all_to_all.14, bf16[5120,32,1,1]{0,1,2,3:T(8,128)(2,1)S(1)} %bitcast.63), kind=kOutput, calls=%fused_computation.18 | convolution fusion | flops 1310720 | bytes 1638912 | tf_op jit(solution)/shard_map/secd,de->sec/dot_general | solution.py:139
  163.2 2.2 %multiply_convert_fusion = bf16[2,32,2,5120]{3,2,1,0:T(2,128)(2,1)} fusion(bf16[2,32,2,5120]{3,2,1,0:T(2,128)(2,1)S(1)} %all_to_all.14, f32[2,32,2]{2,1,0:T(8,128)S(1)} %fusion.34), kind=kLoop, calls=%fused_computation.2 | loop fusion | flops 1966080 | bytes 2621952 | tf_op jit(solution)/shard_map/convert_element_type | solution.py:140
  (10 shorter events, 0.1 us)
Async XLA Ops:
  6.5 81.5 %copy-start = (bf16[1280,1280]{1,0:T(8,128)(2,1)S(1)}, bf16[1280,1280]{1,0:T(8,128)(2,1)}, u32[]{:S(2)}) copy-start(bf16[1280,1280]{1,0:T(8,128)(2,1)} %param.15) | copy-start | bytes 9830404
  6.5 81.5 %all-gather.2.cloned.1.call-start = ((), (), s32[]{:S(2)}) async-start(), calls=%async_computation.3 | async-start | bytes 1638400 | tf_op jit(solution)/shard_map/all_gather | solution.py:94
  37.5 0.8 copy-start.2
  57.1 43.2 %reduce-scatter.2.cloned.1.call-start = ((), (), s32[]{:S(2)}) async-start(), calls=%async_computation.4 | async-start | bytes 1966080 | tf_op jit(solution)/shard_map/reduce_scatter | solution.py:96
  92.3 13.0 %copy-start.6 = (s32[64]{0:T(128)S(1)}, s32[64]{0:T(128)}, u32[]{:S(2)}) copy-start(s32[64]{0:T(128)} %param.19) | copy-start | bytes 772
  92.3 13.0 %copy-start.3 = (bf16[5120]{0:T(1024)(128)(2,1)S(1)}, bf16[5120]{0:T(1024)(128)(2,1)}, u32[]{:S(2)}) copy-start(bf16[5120]{0:T(1024)(128)(2,1)} %param.16) | copy-start | bytes 30724
  92.3 13.0 %copy-start.4 = (s32[1,64,1]{1,2,0:T(1,128)S(1)}, s32[1,64,1]{1,2,0:T(1,128)}, u32[]{:S(2)}) copy-start(s32[1,64,1]{1,2,0:T(1,128)} %param.18) | copy-start | bytes 772
  100.3 22.7 %all-to-all-start = ((bf16[4,64,1280]{2,1,0:T(8,128)(2,1)}), bf16[4,64,1280]{2,1,0:T(8,128)(2,1)}, u32[]{:S(2)}, u32[]{:S(2)}) async-start(bf16[4,64,1280]{2,1,0:T(8,128)(2,1)} %bitcast.55), calls=%async_computation.1 | async-start | bytes 1310720 | tf_op jit(solution)/shard_map/all_to_all | solution.py:104
  125.0 1.1 copy-start.1
  131.9 19.7 %copy-start.5 = (bf16[5120,32]{0,1:T(8,128)(2,1)S(1)}, bf16[5120,32]{0,1:T(8,128)(2,1)}, u32[]{:S(2)}) copy-start(bf16[5120,32]{0,1:T(8,128)(2,1)} %param.17) | copy-start | bytes 983044
Sparse Core Ops, SparseCore 0:
  57.2 30.8 all-gather.1
  92.4 7.7 reduce-scatter.1
where the time goes:
time: 173 us; the launch traced here: 172 us
  blocking collectives  60.6 us (35%)
  waiting for transfers between devices  56.3 us (33%)
  matrix products  19.5 us (11%)
  between operations  13.6 us (8%)
  local copies, waits for them, and re-layouts  12.5 us (7%)
  starting transfers between devices  5.02 us (3%)
  other arithmetic  4.83 us (3%)
    all_gather x1, waiting for transfers between devices, on_device(): gathered = lax.all_gather(attn_rows, 'ctx', axis=1, tiled=True)  30.9 us
    all_to_all x1, blocking collectives, on_device(): lax.all_to_all(outgoing, 'exp', split_axis=0, concat_axis=0, tiled=True)  19.7 us
    all_to_all x1, waiting for transfers between devices, on_device(): lax.all_to_all(own_columns.astype(jnp.bfloat16), 'ctx', split_axis=0, con...  17.4 us
    all_gather x1, blocking collectives, on_device(): value_piece = lax.all_gather(values, 'ctx', axis=1, tiled=True)  14.1 us
    all_gather x1, blocking collectives, on_device(): key_piece = lax.all_gather(key_states, 'ctx', axis=1, tiled=True)  13.9 us
    all_gather x1, blocking collectives, on_device(): doc_piece = lax.all_gather(doc_ids, 'ctx', axis=1, tiled=True)  12.9 us
    dot_general x1, matrix products, on_device(): jnp.einsum('secd,de->sec', arrived, router, preferred_element_type=jnp.fl...  11.5 us
    reduce_scatter x1, waiting for transfers between devices, on_device(): lax.psum_scatter(jnp.dot(gathered, out_proj, preferred_element_type=jnp.f...  7.95 us
  transfers between devices with their start and end apart: 3, of which 3 were waited for; matrix products, arithmetic and copies ran while one was open for 0% of the time, Pallas kernels for 0%

commit v1 on v0

v1 whole, which is shorter than its diff:
```python
import functools
import math

import jax
import jax.numpy as jnp
from jax import lax
from jax.experimental import pallas as pl
from jax.experimental.pallas import tpu as pltpu
from jax.sharding import PartitionSpec as P

CAP = 2
EPSILON = 1e-05
MESH = pl.DeviceIdType.MESH


def kernel(
    sizes,
    q_ref,
    kv_ref,
    doc_ref,
    residual_hbm,
    weight_hbm,
    gain_ref,
    router_ref,
    ids_ref,
    keep_ref,
    out_ref,
    kv_in,
    doc_in,
    attn,
    weight,
    residual,
    product,
    part_out,
    part_in,
    res_out,
    res_in,
    slot_out,
    slot_in,
    load_sem,
    kv_send,
    kv_recv,
    doc_send,
    doc_recv,
    right_send,
    left_send,
    attn_recv,
    part_send,
    part_recv,
    res_send,
    res_recv,
    slot_send,
    slot_recv,
):
    ctx_count, exp_count, back = sizes
    heads, tokens, size = q_ref.shape
    groups = kv_ref.shape[0]
    ratio = heads // groups
    half = tokens // 2
    columns = weight.shape[1]
    depth = weight.shape[0] // groups
    slots = slot_in.shape[2]
    me = lax.axis_index("ctx")
    mine = lax.axis_index("exp")
    core = lax.axis_index("tp")

    load_weight = pltpu.make_async_copy(weight_hbm, weight, load_sem.at[0])
    load_weight.start()
    aligned = columns % 128 == 0
    load_residual = []
    for block in range(ctx_count):
        there = slice(block * columns, (block + 1) * columns)
        load_residual.append(
            pltpu.make_async_copy(
                residual_hbm.at[:, there] if aligned else residual_hbm.at[block],
                residual.at[block],
                load_sem.at[1 + block],
            )
        )
        load_residual[-1].start()

    barrier = pltpu.get_barrier_semaphore()
    for shift in range(1, ctx_count):
        pl.semaphore_signal(
            barrier,
            inc=1,
            device_id={"ctx": lax.rem(me + shift, ctx_count)},
            device_id_type=MESH,
        )
    for shift in range(1, exp_count):
        pl.semaphore_signal(
            barrier,
            inc=1,
            device_id={"exp": lax.rem(mine + shift, exp_count)},
            device_id_type=MESH,
        )
    pl.semaphore_signal(barrier, inc=1, device_id={"tp": 1 - core}, device_id_type=MESH)

    row = lax.broadcasted_iota(jnp.int32, (half, half), 0)
    lane = lax.broadcasted_iota(jnp.int32, (half, half), 1)
    ids_row = ids_ref[...]
    ids_column = jnp.sum(jnp.where(row == lane, ids_row, 0), axis=1, keepdims=True)
    ranking = jnp.sum(
        jnp.where((ids_column == ids_row) & (row < lane), 1, 0), axis=0, keepdims=True
    )
    experts = keep_ref.shape[1]
    square_row = lax.broadcasted_iota(jnp.int32, (experts, experts), 0)
    square_lane = lax.broadcasted_iota(jnp.int32, (experts, experts), 1)
    keep_column = jnp.sum(
        jnp.where(square_row == square_lane, keep_ref[...], 0), axis=1, keepdims=True
    )
    expert_row = lax.broadcasted_iota(jnp.int32, (experts, half), 0)
    limits = jnp.sum(jnp.where(expert_row == ids_row, keep_column, 0), axis=0, keepdims=True)
    target = jnp.where(ranking < limits, ids_row * CAP + ranking, -1)
    slot_row = lax.broadcasted_iota(jnp.int32, (slots, half), 0)

    pl.semaphore_wait(barrier, ctx_count + exp_count - 1)

    def kv_copy(group, shift):
        return pltpu.make_async_remote_copy(
            src_ref=kv_ref.at[group],
            dst_ref=kv_in.at[group, shift - 1],
            send_sem=kv_send.at[group, shift - 1],
            recv_sem=kv_recv.at[group, shift - 1],
            device_id={"ctx": lax.rem(me + shift, ctx_count)},
            device_id_type=MESH,
        )

    def doc_copy(shift):
        return pltpu.make_async_remote_copy(
            src_ref=doc_ref,
            dst_ref=doc_in.at[shift - 1],
            send_sem=doc_send.at[shift - 1],
            recv_sem=doc_recv.at[shift - 1],
            device_id={"ctx": lax.rem(me + shift, ctx_count)},
            device_id_type=MESH,
        )

    for shift in range(1, back + 1):

        @pl.when(me + shift < ctx_count)
        def _(shift=shift):
            doc_copy(shift).start()

    for group in range(groups):
        for shift in range(1, back + 1):

            @pl.when(me + shift < ctx_count)
            def _(group=group, shift=shift):
                kv_copy(group, shift).start()

    for shift in range(1, back + 1):

        @pl.when(me < shift)
        def _(shift=shift):
            doc_in[shift - 1] = jnp.full(doc_in.shape[1:], -1, jnp.int32)
            for group in range(groups):
                kv_in[group, shift - 1] = jnp.zeros(kv_in.shape[2:], kv_in.dtype)

        @pl.when(me >= shift)
        def _(shift=shift):
            doc_copy(shift).wait_recv()

    square = lax.broadcasted_iota(jnp.int32, (tokens, tokens), 0)
    across = lax.broadcasted_iota(jnp.int32, (tokens, tokens), 1)
    doc_row = doc_ref[...]
    doc_column = jnp.sum(jnp.where(square == across, doc_row, 0), axis=1, keepdims=True)
    allowed = [(across <= square) & (doc_row == doc_column)]
    for shift in range(1, back + 1):
        allowed.append(doc_in[shift - 1] == doc_column)
    allowed = jnp.concatenate(
        [jnp.where(piece, 1.0, 0.0) for piece in allowed], axis=1
    )
    allowed = allowed > 0.5
    scale = 1.0 / math.sqrt(size)

    def attn_copy(block, group, rightward):
        to = me + 1 if rightward else me - 1
        sends = right_send if rightward else left_send
        return pltpu.make_async_remote_copy(
            src_ref=attn.at[block, group],
            dst_ref=attn.at[block, group],
            send_sem=sends.at[block, group],
            recv_sem=attn_recv.at[block, group],
            device_id={"ctx": lax.rem(to + ctx_count, ctx_count)},
            device_id_type=MESH,
        )

    for group in range(groups):
        for shift in range(1, back + 1):

            @pl.when(me >= shift)
            def _(group=group, shift=shift):
                kv_copy(group, shift).wait_recv()

        keys = jnp.concatenate(
            [kv_ref[group, 0]] + [kv_in[group, shift, 0] for shift in range(back)], axis=0
        )
        vals = jnp.concatenate(
            [kv_ref[group, 1]] + [kv_in[group, shift, 1] for shift in range(back)], axis=0
        )
        for head in range(ratio):
            scores = (
                lax.dot_general(
                    q_ref[group * ratio + head],
                    keys,
                    (((1,), (1,)), ((), ())),
                    preferred_element_type=jnp.float32,
                )
                * scale
            )
            masked = jnp.where(allowed, scores, -1e30)
            highest = jnp.max(masked, axis=1, keepdims=True)
            weights = jnp.where(allowed, jnp.exp(masked - highest), 0.0)
            totals = jnp.sum(weights, axis=1, keepdims=True)
            mixed = jnp.dot(weights.astype(jnp.bfloat16), vals, preferred_element_type=jnp.float32)
            attn[me, group, :, head * size : (head + 1) * size] = (mixed / totals).astype(
                jnp.bfloat16
            )

        @pl.when(me < ctx_count - 1)
        def _(group=group):
            attn_copy(me, group, True).start()

        @pl.when(me > 0)
        def _(group=group):
            attn_copy(me, group, False).start()

    def part_copy(block):
        return pltpu.make_async_remote_copy(
            src_ref=part_out.at[block],
            dst_ref=part_in.at[block],
            send_sem=part_send.at[block],
            recv_sem=part_recv.at[block],
            device_id={"tp": 1 - core},
            device_id_type=MESH,
        )

    def res_copy(block, peer):
        return pltpu.make_async_remote_copy(
            src_ref=res_out.at[block],
            dst_ref=res_in.at[me],
            send_sem=res_send.at[block],
            recv_sem=res_recv.at[peer],
            device_id={"ctx": block},
            device_id_type=MESH,
        )

    def slot_copy(shift, block, peer):
        return pltpu.make_async_remote_copy(
            src_ref=slot_out.at[shift - 1, block],
            dst_ref=slot_in.at[mine, block],
            send_sem=slot_send.at[shift - 1, block],
            recv_sem=slot_recv.at[peer, block],
            device_id={"exp": lax.rem(mine + shift, exp_count)},
            device_id_type=MESH,
        )

    tile = math.gcd(columns, 256)

    def project(block):
        for first in range(0, columns, tile):
            total = None
            for group in range(groups):
                term = jnp.dot(
                    attn[block, group],
                    weight[group * depth : (group + 1) * depth, first : first + tile],
                    preferred_element_type=jnp.float32,
                )
                total = term if total is None else total + term
            product[block, 0, :, first : first + tile] = total[:half]
            product[block, 1, :, first : first + tile] = total[half:]
        part_out[block] = product[block, 1 - core].astype(jnp.bfloat16)
        part_copy(block).start()

    def finish(block):
        part_copy(block).wait_recv()
        return (product[block, core] + part_in[block].astype(jnp.float32)).astype(jnp.bfloat16)

    def place(block):
        hidden = (
            residual[block].astype(jnp.float32)
            + res_in[block].astype(jnp.float32)
        ).astype(jnp.bfloat16)
        for shift in range(exp_count):
            peer = lax.rem(mine + shift, exp_count)
            table = (slot_row + peer * slots == target).astype(jnp.bfloat16)
            chosen = jnp.dot(table, hidden, preferred_element_type=jnp.float32).astype(
                jnp.bfloat16
            )
            if shift == 0:
                slot_in[mine, block] = chosen
            else:
                slot_out[shift - 1, block] = chosen
                slot_copy(shift, block, mine).start()

    load_weight.wait()
    project(me)
    for load in load_residual:
        load.wait()
    res_in[me] = finish(me)
    place(me)

    def step(distance, carry):
        left, right = me - distance, me + distance
        inside = distance < ctx_count
        has_left = (left >= 0) & inside
        has_right = (right < ctx_count) & inside

        @pl.when(has_left)
        def _():
            for group in range(groups):
                attn_copy(left, group, True).wait_recv()

                @pl.when(me < ctx_count - 1)
                def _():
                    attn_copy(left, group, True).start()

        @pl.when(has_right)
        def _():
            for group in range(groups):
                attn_copy(right, group, False).wait_recv()

                @pl.when(me > 0)
                def _():
                    attn_copy(right, group, False).start()

        for block, has in ((left, has_left), (right, has_right)):

            @pl.when(has)
            def _(block=block):
                project(block)

        for block, has in ((left, has_left), (right, has_right)):

            @pl.when(has)
            def _(block=block):
                res_out[block] = finish(block)
                res_copy(block, me).start()

        for block, ok in (
            (left + 1, (left + 1 >= 0) & (distance >= 2)),
            (right - 1, (right - 1 < ctx_count) & (distance >= 2)),
        ):

            @pl.when(ok)
            def _(block=block):
                res_copy(me, block).wait_recv()
                place(block)

        return carry

    lax.fori_loop(1, ctx_count + 1, step, 0)

    spread = lax.broadcasted_iota(jnp.int32, (slots, router_ref.shape[0]), 0) // CAP
    expert = lax.broadcasted_iota(jnp.int32, (slots, router_ref.shape[0]), 1)
    for shift in range(exp_count):
        peer = lax.rem(mine + shift, exp_count)
        if shift:
            for block in range(ctx_count):
                slot_copy(1, block, peer).wait_recv()
        power = 0.0
        for block in range(ctx_count):
            hidden = slot_in[peer, block].astype(jnp.float32)
            power = power + jnp.sum(hidden * hidden, axis=1, keepdims=True)
        factor = lax.rsqrt(power / (columns * ctx_count) + EPSILON)
        logits = 0.0
        for block in range(ctx_count):
            there = slice(block * columns, (block + 1) * columns)
            normed = (
                slot_in[peer, block].astype(jnp.float32)
                * factor
                * gain_ref[:, there].astype(jnp.float32)
            ).astype(jnp.bfloat16)
            slot_in[peer, block] = normed
            logits = logits + lax.dot_general(
                normed,
                router_ref[:, there],
                (((1,), (1,)), ((), ())),
                preferred_element_type=jnp.float32,
            )
        logit = jnp.sum(jnp.where(spread == expert, logits, 0.0), axis=1, keepdims=True)
        gate = jax.nn.sigmoid(logit)
        for block in range(ctx_count):
            out_ref[peer, :, block * columns : (block + 1) * columns] = (
                slot_in[peer, block].astype(jnp.float32) * gate
            ).astype(jnp.bfloat16)

    for shift in range(1, back + 1):

        @pl.when(me + shift < ctx_count)
        def _(shift=shift):
            doc_copy(shift).wait_send()
            for group in range(groups):
                kv_copy(group, shift).wait_send()

    def drain(block, carry):
        part_copy(block).wait_send()
        for shift in range(1, exp_count):
            slot_copy(shift, block, mine).wait_send()

        @pl.when(block != me)
        def _():
            res_copy(block, me).wait_send()

        for group in range(groups):

            @pl.when((block <= me) & (me < ctx_count - 1))
            def _(group=group):
                attn_copy(block, group, True).wait_send()

            @pl.when((block >= me) & (me > 0))
            def _(group=group):
                attn_copy(block, group, False).wait_send()

        return carry

    lax.fori_loop(0, ctx_count, drain, 0)


def on_device(
    queries,
    key_states,
    values,
    doc_ids,
    residual,
    out_proj,
    norm_gain,
    router,
    expert_ids,
    keep_counts,
):
    tokens, heads, size = queries.shape[1:]
    groups = key_states.shape[2]
    ctx_count = lax.axis_size("ctx")
    exp_count = lax.axis_size("exp")
    features, columns = out_proj.shape
    half = residual.shape[1]
    width = residual.shape[2]
    experts = keep_counts.shape[0]
    slots = experts // exp_count * CAP
    longest = tokens * ctx_count // 2
    back = min(ctx_count - 1, -(-(longest - 1) // tokens))
    kv = jnp.stack([key_states[0], values[0]]).transpose(2, 0, 1, 3)
    vmem = pl.BlockSpec(memory_space=pltpu.VMEM)
    hbm = pl.BlockSpec(memory_space=pl.ANY)
    bf16, f32 = jnp.bfloat16, jnp.float32
    dma = pltpu.SemaphoreType.DMA
    n = ctx_count
    stream = residual[0]
    if columns % 128:
        stream = stream.reshape(half, ctx_count, columns).transpose(1, 0, 2)
    out = pl.pallas_call(
        functools.partial(kernel, (ctx_count, exp_count, back)),
        out_shape=jax.ShapeDtypeStruct((exp_count, slots, width), bf16),
        in_specs=[vmem, vmem, vmem, hbm, hbm, vmem, vmem, vmem, vmem],
        out_specs=vmem,
        scratch_shapes=[
            pltpu.VMEM((groups, back, 2, tokens, size), bf16),
            pltpu.VMEM((back, 1, tokens), jnp.int32),
            pltpu.VMEM((n, groups, tokens, features // groups), bf16),
            pltpu.VMEM((features, columns), bf16),
            pltpu.VMEM((n, half, columns), bf16),
            pltpu.VMEM((n, 2, half, columns), f32),
            pltpu.VMEM((n, half, columns), bf16),
            pltpu.VMEM((n, half, columns), bf16),
            pltpu.VMEM((n, half, columns), bf16),
            pltpu.VMEM((n, half, columns), bf16),
            pltpu.VMEM((exp_count - 1, n, slots, columns), bf16),
            pltpu.VMEM((exp_count, n, slots, columns), bf16),
            dma((1 + n,)),
            dma((groups, back)),
            dma((groups, back)),
            dma((back,)),
            dma((back,)),
            dma((n, groups)),
            dma((n, groups)),
            dma((n, groups)),
            dma((n,)),
            dma((n,)),
            dma((n,)),
            dma((n,)),
            dma((exp_count - 1, n)),
            dma((exp_count, n)),
        ],
        compiler_params=pltpu.CompilerParams(collective_id=0, has_side_effects=True),
    )(
        queries[0].transpose(1, 0, 2),
        kv,
        doc_ids,
        stream,
        out_proj,
        norm_gain.reshape(1, width),
        router.T,
        expert_ids.reshape(1, half),
        keep_counts.reshape(1, experts),
    )
    return out.reshape(exp_count, experts // exp_count, CAP, width)


def solution(mesh):
    placed = (
        P(("groups", "exp"), "ctx", "tp", None),
        P(("groups", "exp"), "ctx", "tp", None),
        P(("groups", "exp"), "ctx", "tp", None),
        P(("groups", "exp"), "ctx"),
        P(("groups", "exp"), ("ctx", "tp"), None),
        P("tp", "ctx"),
        P(),
        P(None, "exp"),
        P(("groups", "exp"), ("ctx", "tp"), None),
        P("groups"),
    )
    return jax.shard_map(
        on_device,
        mesh=mesh,
        in_specs=placed,
        out_specs=P(("groups", "ctx", "tp"), "exp", None, None),
        check_vma=False,
    )
```

time: 173 us -> 67.8 us (0.39)
  blocking collectives: 60.6 us -> 0 us
  Pallas kernels: 0 us -> 59.9 us
  waiting for transfers between devices: 56.3 us -> 0 us
  matrix products: 19.5 us -> 0 us
  between operations: 13.6 us -> 0.02 us
  local copies, waits for them, and re-layouts: 12.5 us -> 6.88 us
  starting transfers between devices: 5.02 us -> 0 us
  other arithmetic: 4.83 us -> 0.67 us
    pallas_call x0 -> x1, Pallas kernels: none -> 59.9 us  [on_device(): pl.pallas_call(functools.partial(kernel, (ctx_count, exp_count, back)), o...]
    all_gather x3 -> x0, blocking collectives: 40.9 us -> none  [the longest x1 14.1 us: on_device(): value_piece = lax.all_gather(values, 'ctx', axis=1, tiled=True)]
    all_gather x1 -> x0, waiting for transfers between devices: 30.9 us -> none  [on_device(): gathered = lax.all_gather(attn_rows, 'ctx', axis=1, tiled=True)]
    all_to_all x1 -> x0, blocking collectives: 19.7 us -> none  [on_device(): lax.all_to_all(outgoing, 'exp', split_axis=0, concat_axis=0, tiled=True)]
    dot_general x6 -> x0, matrix products: 19.5 us -> none  [the longest x1 11.5 us: on_device(): jnp.einsum('secd,de->sec', arrived, router, preferred_element_type=jnp.fl...]
    all_to_all x1 -> x0, waiting for transfers between devices: 17.4 us -> none  [on_device(): lax.all_to_all(own_columns.astype(jnp.bfloat16), 'ctx', split_axis=0, con...]
    reduce_scatter x1 -> x0, waiting for transfers between devices: 7.95 us -> none  [on_device(): lax.psum_scatter(jnp.dot(gathered, out_proj, preferred_element_type=jnp.f...]
    all_to_all x1 -> x0, starting transfers between devices: 4.98 us -> none  [on_device(): lax.all_to_all(own_columns.astype(jnp.bfloat16), 'ctx', split_axis=0, con...]
  transfers between devices with their start and end apart: 3 -> 0, of which waited for: 3 -> 0; matrix products, arithmetic and copies ran while one was open for 0% -> 0% of each run, Pallas kernels for 0% -> 0%
where the time goes in v1:
time: 67.8 us; the launch traced here: 67.5 us
  Pallas kernels  59.9 us (88%)
  local copies, waits for them, and re-layouts  6.88 us (10%)
    pallas_call x1, Pallas kernels, on_device(): pl.pallas_call(functools.partial(kernel, (ctx_count, exp_count, back)), o...  59.9 us
    reshape x1, local copies, waits for them, and re-layouts, on_device(): return out.reshape(exp_count, experts // exp_count, CAP, width)  3.86 us
    unnamed x2, local copies, waits for them, and re-layouts  1.7 us

profile of v1, /device:TPU:0, one launch (start us, length us, event | category | flops | bytes accessed | tf_op | source)
XLA Modules:
  0.0 67.5 jit_solution(18086561519903950089)
XLA Ops:
  0.0 1.3 %reshape.12.gain_ref = bf16[1,5120]{1,0:T(2,128)(2,1)} reshape(bf16[5120]{0:T(1024)(128)(2,1)} %param.16) | data formatting | bytes 20480 | tf_op jit(solution)/shard_map/reshape | solution.py:493
  1.3 0.8 %copy.11 = bf16[1,128,2,128]{3,1,0,2:T(8,128)(2,1)S(1)} copy(bf16[1,128,2,128]{3,2,1,0:T(2,128)(2,1)} %param.11) | data formatting | bytes 131072 | tf_op args[1]
  2.2 0.9 %copy.12 = bf16[1,128,2,128]{3,1,0,2:T(8,128)(2,1)S(1)} copy(bf16[1,128,2,128]{3,2,1,0:T(2,128)(2,1)} %param.12) | data formatting | bytes 131072 | tf_op args[2]
  3.0 0.7 maximum_bitcast_fusion.kv_ref
  3.7 59.9 %shard_map.100 = bf16[2,64,5120]{2,1,0:T(8,128)(2,1)} custom-call(bf16[10,128,128]{2,1,0:T(8,128)(2,1)} %bitcast.10, bf16[2,2,128,128]{3,2,1,0:T(8,128)(2,1)} %maximum_bitcast_fusion.kv_ref, s32[1,128]{1,0:T(1,128)} %doc_ref.1, bf16[64,5120]{1,0:T(8,128)(2,1)} %bitcast.9, bf16[1280,1280]{1,0:T(8,128)(2,1)} %weight_hbm.1, bf16[1,5120]{1,0:T(2,128)(2,1)} %reshape.12.gain_ref, ...), custom_call_target="tpu_custom_call" | custom-call | tf_op jit(solution)/shard_map/pallas_call | solution.py:453
  63.6 3.9 %reshape.15 = bf16[2,32,2,5120]{3,2,1,0:T(2,128)(2,1)} reshape(bf16[2,64,5120]{2,1,0:T(8,128)(2,1)} %shard_map.100) | data formatting | bytes 2621440 | tf_op jit(solution)/shard_map/reshape | solution.py:498

commit v2 on v1

--- a/solution.py
+++ b/solution.py
@@ -16,7 +16,8 @@
 def kernel(
     sizes,
     q_ref,
-    kv_ref,
+    key_ref,
+    value_ref,
     doc_ref,
     residual_hbm,
     weight_hbm,
@@ -25,7 +26,10 @@
     ids_ref,
     keep_ref,
     out_ref,
+    kv_out,
     kv_in,
+    gain,
+    tally,
     doc_in,
     attn,
     weight,
@@ -52,14 +56,15 @@
     slot_send,
     slot_recv,
 ):
-    ctx_count, exp_count, back = sizes
+    ctx_count, exp_count, back, pieces = sizes
     heads, tokens, size = q_ref.shape
-    groups = kv_ref.shape[0]
+    groups = kv_out.shape[0]
     ratio = heads // groups
     half = tokens // 2
     columns = weight.shape[1]
     depth = weight.shape[0] // groups
-    slots = slot_in.shape[2]
+    slots = slot_in.shape[3]
+    part = columns // pieces
     me = lax.axis_index("ctx")
     mine = lax.axis_index("exp")
     core = lax.axis_index("tp")
@@ -95,6 +100,44 @@
             device_id_type=MESH,
         )
     pl.semaphore_signal(barrier, inc=1, device_id={"tp": 1 - core}, device_id_type=MESH)
+
+    for group in range(groups):
+        kv_out[group, 0] = key_ref[:, group, :]
+        kv_out[group, 1] = value_ref[:, group, :]
+
+    pl.semaphore_wait(barrier, ctx_count + exp_count - 1)
+
+    def kv_copy(group, shift):
+        return pltpu.make_async_remote_copy(
+            src_ref=kv_out.at[group] if shift == 1 else kv_in.at[group, shift - 2],
+            dst_ref=kv_in.at[group, shift - 1],
+            send_sem=kv_send.at[group, shift - 1],
+            recv_sem=kv_recv.at[group, shift - 1],
+            device_id={"ctx": lax.rem(me + 1, ctx_count)},
+            device_id_type=MESH,
+        )
+
+    def doc_copy(shift):
+        return pltpu.make_async_remote_copy(
+            src_ref=doc_ref,
+            dst_ref=doc_in.at[shift - 1],
+            send_sem=doc_send.at[shift - 1],
+            recv_sem=doc_recv.at[shift - 1],
+            device_id={"ctx": lax.rem(me + shift, ctx_count)},
+            device_id_type=MESH,
+        )
+
+    for shift in range(1, back + 1):
+
+        @pl.when(me + shift < ctx_count)
+        def _(shift=shift):
+            doc_copy(shift).start()
+
+    for group in range(groups):
+
+        @pl.when(me + 1 < ctx_count)
+        def _(group=group):
+            kv_copy(group, 1).start()
 
     row = lax.broadcasted_iota(jnp.int32, (half, half), 0)
     lane = lax.broadcasted_iota(jnp.int32, (half, half), 1)
@@ -114,40 +157,9 @@
     target = jnp.where(ranking < limits, ids_row * CAP + ranking, -1)
     slot_row = lax.broadcasted_iota(jnp.int32, (slots, half), 0)
 
-    pl.semaphore_wait(barrier, ctx_count + exp_count - 1)
-
-    def kv_copy(group, shift):
-        return pltpu.make_async_remote_copy(
-            src_ref=kv_ref.at[group],
-            dst_ref=kv_in.at[group, shift - 1],
-            send_sem=kv_send.at[group, shift - 1],
-            recv_sem=kv_recv.at[group, shift - 1],
-            device_id={"ctx": lax.rem(me + shift, ctx_count)},
-            device_id_type=MESH,
-        )
-
-    def doc_copy(shift):
-        return pltpu.make_async_remote_copy(
-            src_ref=doc_ref,
-            dst_ref=doc_in.at[shift - 1],
-            send_sem=doc_send.at[shift - 1],
-            recv_sem=doc_recv.at[shift - 1],
-            device_id={"ctx": lax.rem(me + shift, ctx_count)},
-            device_id_type=MESH,
-        )
-
-    for shift in range(1, back + 1):
-
-        @pl.when(me + shift < ctx_count)
-        def _(shift=shift):
-            doc_copy(shift).start()
-
-    for group in range(groups):
-        for shift in range(1, back + 1):
-
-            @pl.when(me + shift < ctx_count)
-            def _(group=group, shift=shift):
-                kv_copy(group, shift).start()
+    wide = gain_ref[...].astype(jnp.float32)
+    for line in range(wide.shape[0]):
+        gain[:, line * 128 : (line + 1) * 128] = wide[line : line + 1]
 
     for shift in range(1, back + 1):
 
@@ -192,12 +204,17 @@
             @pl.when(me >= shift)
             def _(group=group, shift=shift):
                 kv_copy(group, shift).wait_recv()
+                if shift < back:
+
+                    @pl.when(me + 1 < ctx_count)
+                    def _():
+                        kv_copy(group, shift + 1).start()
 
         keys = jnp.concatenate(
-            [kv_ref[group, 0]] + [kv_in[group, shift, 0] for shift in range(back)], axis=0
+            [kv_out[group, 0]] + [kv_in[group, shift, 0] for shift in range(back)], axis=0
         )
         vals = jnp.concatenate(
-            [kv_ref[group, 1]] + [kv_in[group, shift, 1] for shift in range(back)], axis=0
+            [kv_out[group, 1]] + [kv_in[group, shift, 1] for shift in range(back)], axis=0
         )
         for head in range(ratio):
             scores = (
@@ -226,80 +243,85 @@
         def _(group=group):
             attn_copy(me, group, False).start()
 
-    def part_copy(block):
+    def part_copy(block, piece):
         return pltpu.make_async_remote_copy(
-            src_ref=part_out.at[block],
-            dst_ref=part_in.at[block],
-            send_sem=part_send.at[block],
-            recv_sem=part_recv.at[block],
+            src_ref=part_out.at[block, piece],
+            dst_ref=part_in.at[block, piece],
+            send_sem=part_send.at[block, piece],
+            recv_sem=part_recv.at[block, piece],
             device_id={"tp": 1 - core},
             device_id_type=MESH,
         )
 
-    def res_copy(block, peer):
+    def res_copy(block, peer, piece):
         return pltpu.make_async_remote_copy(
-            src_ref=res_out.at[block],
-            dst_ref=res_in.at[me],
-            send_sem=res_send.at[block],
-            recv_sem=res_recv.at[peer],
+            src_ref=res_out.at[block, piece],
+            dst_ref=res_in.at[me, piece],
+            send_sem=res_send.at[block, piece],
+            recv_sem=res_recv.at[peer, piece],
             device_id={"ctx": block},
             device_id_type=MESH,
         )
 
-    def slot_copy(shift, block, peer):
+    def slot_copy(shift, block, peer, piece):
         return pltpu.make_async_remote_copy(
-            src_ref=slot_out.at[shift - 1, block],
-            dst_ref=slot_in.at[mine, block],
-            send_sem=slot_send.at[shift - 1, block],
-            recv_sem=slot_recv.at[peer, block],
+            src_ref=slot_out.at[shift - 1, block, piece],
+            dst_ref=slot_in.at[mine, block, piece],
+            send_sem=slot_send.at[shift - 1, block, piece],
+            recv_sem=slot_recv.at[peer, block, piece],
             device_id={"exp": lax.rem(mine + shift, exp_count)},
             device_id_type=MESH,
         )
 
-    tile = math.gcd(columns, 256)
-
-    def project(block):
-        for first in range(0, columns, tile):
+    tile = math.gcd(part, 128)
+
+    def project(block, piece):
+        for first in range(0, part, tile):
+            there = slice(piece * part + first, piece * part + first + tile)
             total = None
             for group in range(groups):
                 term = jnp.dot(
                     attn[block, group],
-                    weight[group * depth : (group + 1) * depth, first : first + tile],
+                    weight[group * depth : (group + 1) * depth, there],
                     preferred_element_type=jnp.float32,
                 )
                 total = term if total is None else total + term
-            product[block, 0, :, first : first + tile] = total[:half]
-            product[block, 1, :, first : first + tile] = total[half:]
-        part_out[block] = product[block, 1 - core].astype(jnp.bfloat16)
-        part_copy(block).start()
-
-    def finish(block):
-        part_copy(block).wait_recv()
-        return (product[block, core] + part_in[block].astype(jnp.float32)).astype(jnp.bfloat16)
-
-    def place(block):
+            product[block, piece, 0, :, first : first + tile] = total[:half]
+            product[block, piece, 1, :, first : first + tile] = total[half:]
+        part_out[block, piece] = product[block, piece, 1 - core].astype(jnp.bfloat16)
+        part_copy(block, piece).start()
+
+    def finish(block, piece):
+        part_copy(block, piece).wait_recv()
+        return (
+            product[block, piece, core] + part_in[block, piece].astype(jnp.float32)
+        ).astype(jnp.bfloat16)
+
+    def place(block, piece):
         hidden = (
-            residual[block].astype(jnp.float32)
-            + res_in[block].astype(jnp.float32)
+            residual[block, :, piece * part : (piece + 1) * part].astype(jnp.float32)
+            + res_in[block, piece].astype(jnp.float32)
         ).astype(jnp.bfloat16)
-        for shift in range(exp_count):
+        for shift in (*range(1, exp_count), 0):
             peer = lax.rem(mine + shift, exp_count)
             table = (slot_row + peer * slots == target).astype(jnp.bfloat16)
             chosen = jnp.dot(table, hidden, preferred_element_type=jnp.float32).astype(
                 jnp.bfloat16
             )
             if shift == 0:
-                slot_in[mine, block] = chosen
+                slot_in[mine, block, piece] = chosen
             else:
-                slot_out[shift - 1, block] = chosen
-                slot_copy(shift, block, mine).start()
+                slot_out[shift - 1, block, piece] = chosen
+                slot_copy(shift, block, mine, piece).start()
 
     load_weight.wait()
-    project(me)
+    for piece in range(pieces):
+        project(me, piece)
     for load in load_residual:
         load.wait()
-    res_in[me] = finish(me)
-    place(me)
+    for piece in range(pieces):
+        res_in[me, piece] = finish(me, piece)
+        place(me, piece)
 
     def step(distance, carry):
         left, right = me - distance, me + distance
@@ -325,28 +347,31 @@
                 def _():
                     attn_copy(right, group, False).start()
 
-        for block, has in ((left, has_left), (right, has_right)):
-
-            @pl.when(has)
-            def _(block=block):
-                project(block)
-
-        for block, has in ((left, has_left), (right, has_right)):
-
-            @pl.when(has)
-            def _(block=block):
-                res_out[block] = finish(block)
-                res_copy(block, me).start()
-
-        for block, ok in (
-            (left + 1, (left + 1 >= 0) & (distance >= 2)),
-            (right - 1, (right - 1 < ctx_count) & (distance >= 2)),
-        ):
-
-            @pl.when(ok)
-            def _(block=block):
-                res_copy(me, block).wait_recv()
-                place(block)
+        for piece in range(pieces):
+            for block, has in ((left, has_left), (right, has_right)):
+
+                @pl.when(has)
+                def _(block=block):
+                    project(block, piece)
+
+        for piece in range(pieces):
+            for block, has in ((left, has_left), (right, has_right)):
+
+                @pl.when(has)
+                def _(block=block):
+                    res_out[block, piece] = finish(block, piece)
+                    res_copy(block, me, piece).start()
+
+        for piece in range(pieces):
+            for block, ok in (
+                (left + 1, (left + 1 >= 0) & (distance >= 2)),
+                (right - 1, (right - 1 < ctx_count) & (distance >= 2)),
+            ):
+
+                @pl.when(ok)
+                def _(block=block):
+                    res_copy(me, block, piece).wait_recv()
+                    place(block, piece)
 
         return carry
 
@@ -356,52 +381,76 @@
     expert = lax.broadcasted_iota(jnp.int32, (slots, router_ref.shape[0]), 1)
     for shift in range(exp_count):
         peer = lax.rem(mine + shift, exp_count)
-        if shift:
-            for block in range(ctx_count):
-                slot_copy(1, block, peer).wait_recv()
-        power = 0.0
-        for block in range(ctx_count):
-            hidden = slot_in[peer, block].astype(jnp.float32)
-            power = power + jnp.sum(hidden * hidden, axis=1, keepdims=True)
-        factor = lax.rsqrt(power / (columns * ctx_count) + EPSILON)
+        tally[...] = jnp.zeros_like(tally)
+
+        def absorb(block):
+            for piece in range(pieces):
+                if shift:
+                    slot_copy(1, block, peer, piece).wait_recv()
+                hidden = slot_in[peer, block, piece].astype(jnp.float32)
+                tally[:, :1] += jnp.sum(hidden * hidden, axis=1, keepdims=True)
+
+        absorb(me)
+
+        def gather(distance, carry):
+            @pl.when(me >= distance)
+            def _():
+                absorb(me - distance)
+
+            @pl.when(me + distance < ctx_count)
+            def _():
+                absorb(me + distance)
+
+            return carry
+
+        lax.fori_loop(1, ctx_count, gather, 0)
+        factor = lax.rsqrt(tally[:, :1] / (columns * ctx_count) + EPSILON)
         logits = 0.0
         for block in range(ctx_count):
-            there = slice(block * columns, (block + 1) * columns)
-            normed = (
-                slot_in[peer, block].astype(jnp.float32)
-                * factor
-                * gain_ref[:, there].astype(jnp.float32)
-            ).astype(jnp.bfloat16)
-            slot_in[peer, block] = normed
-            logits = logits + lax.dot_general(
-                normed,
-                router_ref[:, there],
-                (((1,), (1,)), ((), ())),
-                preferred_element_type=jnp.float32,
-            )
+            for piece in range(pieces):
+                first = block * columns + piece * part
+                there = slice(first, first + part)
+                normed = (
+                    slot_in[peer, block, piece].astype(jnp.float32) * factor * gain[:, there]
+                ).astype(jnp.bfloat16)
+                slot_in[peer, block, piece] = normed
+                logits = logits + lax.dot_general(
+                    normed,
+                    router_ref[:, there],
+                    (((1,), (1,)), ((), ())),
+                    preferred_element_type=jnp.float32,
+                )
         logit = jnp.sum(jnp.where(spread == expert, logits, 0.0), axis=1, keepdims=True)
         gate = jax.nn.sigmoid(logit)
         for block in range(ctx_count):
-            out_ref[peer, :, block * columns : (block + 1) * columns] = (
-                slot_in[peer, block].astype(jnp.float32) * gate
-            ).astype(jnp.bfloat16)
+            for piece in range(pieces):
+                first = block * columns + piece * part
+                done = slot_in[peer, block, piece].astype(jnp.float32) * gate
+                out_ref[peer, :, :, first : first + part] = done.reshape(
+                    slots // CAP, CAP, part
+                ).astype(jnp.bfloat16)
 
     for shift in range(1, back + 1):
 
         @pl.when(me + shift < ctx_count)
         def _(shift=shift):
             doc_copy(shift).wait_send()
+
+        @pl.when((me + 1 < ctx_count) & (me + 1 >= shift))
+        def _(shift=shift):
             for group in range(groups):
                 kv_copy(group, shift).wait_send()
 
     def drain(block, carry):
-        part_copy(block).wait_send()
-        for shift in range(1, exp_count):
-            slot_copy(shift, block, mine).wait_send()
+        for piece in range(pieces):
+            part_copy(block, piece).wait_send()
+            for shift in range(1, exp_count):
+                slot_copy(shift, block, mine, piece).wait_send()
 
         @pl.when(block != me)
         def _():
-            res_copy(block, me).wait_send()
+            for piece in range(pieces):
+                res_copy(block, me, piece).wait_send()
 
         for group in range(groups):
 
@@ -441,7 +490,8 @@
     slots = experts // exp_count * CAP
     longest = tokens * ctx_count // 2
     back = min(ctx_count - 1, -(-(longest - 1) // tokens))
-    kv = jnp.stack([key_states[0], values[0]]).transpose(2, 0, 1, 3)
+    pieces = 2
+    part = columns // pieces
     vmem = pl.BlockSpec(memory_space=pltpu.VMEM)
     hbm = pl.BlockSpec(memory_space=pl.ANY)
     bf16, f32 = jnp.bfloat16, jnp.float32
@@ -451,23 +501,26 @@
     if columns % 128:
         stream = stream.reshape(half, ctx_count, columns).transpose(1, 0, 2)
     out = pl.pallas_call(
-        functools.partial(kernel, (ctx_count, exp_count, back)),
-        out_shape=jax.ShapeDtypeStruct((exp_count, slots, width), bf16),
-        in_specs=[vmem, vmem, vmem, hbm, hbm, vmem, vmem, vmem, vmem],
+        functools.partial(kernel, (ctx_count, exp_count, back, pieces)),
+        out_shape=jax.ShapeDtypeStruct((exp_count, slots // CAP, CAP, width), bf16),
+        in_specs=[vmem, vmem, vmem, vmem, hbm, hbm, vmem, vmem, vmem, vmem],
         out_specs=vmem,
         scratch_shapes=[
+            pltpu.VMEM((groups, 2, tokens, size), bf16),
             pltpu.VMEM((groups, back, 2, tokens, size), bf16),
+            pltpu.VMEM((1, width), f32),
+            pltpu.VMEM((slots, 128), f32),
             pltpu.VMEM((back, 1, tokens), jnp.int32),
             pltpu.VMEM((n, groups, tokens, features // groups), bf16),
             pltpu.VMEM((features, columns), bf16),
             pltpu.VMEM((n, half, columns), bf16),
-            pltpu.VMEM((n, 2, half, columns), f32),
-            pltpu.VMEM((n, half, columns), bf16),
-            pltpu.VMEM((n, half, columns), bf16),
-            pltpu.VMEM((n, half, columns), bf16),
-            pltpu.VMEM((n, half, columns), bf16),
-            pltpu.VMEM((exp_count - 1, n, slots, columns), bf16),
-            pltpu.VMEM((exp_count, n, slots, columns), bf16),
+            pltpu.VMEM((n, pieces, 2, half, part), f32),
+            pltpu.VMEM((n, pieces, half, part), bf16),
+            pltpu.VMEM((n, pieces, half, part), bf16),
+            pltpu.VMEM((n, pieces, half, part), bf16),
+            pltpu.VMEM((n, pieces, half, part), bf16),
+            pltpu.VMEM((exp_count - 1, n, pieces, slots, part), bf16),
+            pltpu.VMEM((exp_count, n, pieces, slots, part), bf16),
             dma((1 + n,)),
             dma((groups, back)),
             dma((groups, back)),
@@ -476,26 +529,27 @@
             dma((n, groups)),
             dma((n, groups)),
             dma((n, groups)),
-            dma((n,)),
-            dma((n,)),
-            dma((n,)),
-            dma((n,)),
-            dma((exp_count - 1, n)),
-            dma((exp_count, n)),
+            dma((n, pieces)),
+            dma((n, pieces)),
+            dma((n, pieces)),
+            dma((n, pieces)),
+            dma((exp_count - 1, n, pieces)),
+            dma((exp_count, n, pieces)),
         ],
         compiler_params=pltpu.CompilerParams(collective_id=0, has_side_effects=True),
     )(
         queries[0].transpose(1, 0, 2),
-        kv,
+        key_states[0],
+        values[0],
         doc_ids,
         stream,
         out_proj,
-        norm_gain.reshape(1, width),
+        norm_gain.reshape(width // 128, 128),
         router.T,
         expert_ids.reshape(1, half),
         keep_counts.reshape(1, experts),
     )
-    return out.reshape(exp_count, experts // exp_count, CAP, width)
+    return out
 
 
 def solution(mesh):

time: 67.8 us -> 69.3 us (1.022)
  Pallas kernels: 59.9 us -> 65.9 us
  local copies, waits for them, and re-layouts: 6.88 us -> 3.27 us
    pallas_call x1, Pallas kernels: 59.9 us -> 65.9 us  [on_device(): pl.pallas_call(functools.partial(kernel, (ctx_count, exp_count, back, pie...]
    reshape x2 -> x0, local copies, waits for them, and re-layouts: 5.18 us -> none  [the longest x1 3.86 us: on_device(): return out.reshape(exp_count, experts // exp_count, CAP, width)]
    unnamed x2 -> x1, local copies, waits for them, and re-layouts: 1.7 us -> 3.27 us
where the time goes in v2:
time: 69.3 us; the launch traced here: 69.1 us
  Pallas kernels  65.9 us (95%)
  local copies, waits for them, and re-layouts  3.27 us (5%)
    pallas_call x1, Pallas kernels, on_device(): pl.pallas_call(functools.partial(kernel, (ctx_count, exp_count, back, pie...  65.9 us
    unnamed x1, local copies, waits for them, and re-layouts  3.27 us

profile of v2, /device:TPU:0, one launch (start us, length us, event | category | flops | bytes accessed | tf_op | source)
XLA Modules:
  0.0 69.1 jit_solution(3336940261412699715)
XLA Ops:
  0.0 65.9 %shard_map.100 = bf16[2,32,2,5120]{3,2,1,0:T(2,128)(2,1)} custom-call(bf16[10,128,128]{2,1,0:T(8,128)(2,1)} %bitcast.11, bf16[128,2,128]{2,1,0:T(2,128)(2,1)} %bitcast.13, bf16[128,2,128]{2,1,0:T(2,128)(2,1)} %bitcast.14, s32[1,128]{1,0:T(1,128)} %doc_ref.1, bf16[64,5120]{1,0:T(8,128)(2,1)} %bitcast.10, bf16[1280,1280]{1,0:T(8,128)(2,1)} %weight_hbm.1, ...), custom_call_target="tpu_custom_call" | custom-call | tf_op jit(solution)/shard_map/pallas_call | solution.py:503
  65.9 3.3 %copy.12 = bf16[2,32,2,5120]{3,2,1,0:T(2,128)(2,1)} copy(bf16[2,32,2,5120]{3,2,1,0:T(2,128)(2,1)} %shard_map.100) | data formatting | bytes 2621440

commit v3 on v2

--- a/solution.py
+++ b/solution.py
@@ -109,11 +109,11 @@
 
     def kv_copy(group, shift):
         return pltpu.make_async_remote_copy(
-            src_ref=kv_out.at[group] if shift == 1 else kv_in.at[group, shift - 2],
+            src_ref=kv_out.at[group],
             dst_ref=kv_in.at[group, shift - 1],
             send_sem=kv_send.at[group, shift - 1],
             recv_sem=kv_recv.at[group, shift - 1],
-            device_id={"ctx": lax.rem(me + 1, ctx_count)},
+            device_id={"ctx": lax.rem(me + shift, ctx_count)},
             device_id_type=MESH,
         )
 
@@ -134,10 +134,11 @@
             doc_copy(shift).start()
 
     for group in range(groups):
-
-        @pl.when(me + 1 < ctx_count)
-        def _(group=group):
-            kv_copy(group, 1).start()
+        for shift in range(1, back + 1):
+
+            @pl.when(me + shift < ctx_count)
+            def _(group=group, shift=shift):
+                kv_copy(group, shift).start()
 
     row = lax.broadcasted_iota(jnp.int32, (half, half), 0)
     lane = lax.broadcasted_iota(jnp.int32, (half, half), 1)
@@ -204,11 +205,6 @@
             @pl.when(me >= shift)
             def _(group=group, shift=shift):
                 kv_copy(group, shift).wait_recv()
-                if shift < back:
-
-                    @pl.when(me + 1 < ctx_count)
-                    def _():
-                        kv_copy(group, shift + 1).start()
 
         keys = jnp.concatenate(
             [kv_out[group, 0]] + [kv_in[group, shift, 0] for shift in range(back)], axis=0
@@ -273,7 +269,7 @@
             device_id_type=MESH,
         )
 
-    tile = math.gcd(part, 128)
+    tile = math.gcd(part, 640)
 
     def project(block, piece):
         for first in range(0, part, tile):
@@ -435,9 +431,6 @@
         @pl.when(me + shift < ctx_count)
         def _(shift=shift):
             doc_copy(shift).wait_send()
-
-        @pl.when((me + 1 < ctx_count) & (me + 1 >= shift))
-        def _(shift=shift):
             for group in range(groups):
                 kv_copy(group, shift).wait_send()
 

time: 69.3 us -> 62 us (0.89)
  Pallas kernels: 65.9 us -> 58.5 us
    pallas_call x1, Pallas kernels: 65.9 us -> 58.5 us  [on_device(): pl.pallas_call(functools.partial(kernel, (ctx_count, exp_count, back, pie...]
where the time goes in v3:
time: 62 us; the launch traced here: 61.8 us
  Pallas kernels  58.5 us (94%)
  local copies, waits for them, and re-layouts  3.27 us (5%)
    pallas_call x1, Pallas kernels, on_device(): pl.pallas_call(functools.partial(kernel, (ctx_count, exp_count, back, pie...  58.5 us
    unnamed x1, local copies, waits for them, and re-layouts  3.27 us

profile of v3, /device:TPU:0, one launch (start us, length us, event | category | flops | bytes accessed | tf_op | source)
XLA Modules:
  0.0 61.8 jit_solution(2850476673164226288)
XLA Ops:
  0.0 58.5 %shard_map.100 = bf16[2,32,2,5120]{3,2,1,0:T(2,128)(2,1)} custom-call(bf16[10,128,128]{2,1,0:T(8,128)(2,1)} %bitcast.11, bf16[128,2,128]{2,1,0:T(2,128)(2,1)} %bitcast.13, bf16[128,2,128]{2,1,0:T(2,128)(2,1)} %bitcast.14, s32[1,128]{1,0:T(1,128)} %doc_ref.1, bf16[64,5120]{1,0:T(8,128)(2,1)} %bitcast.10, bf16[1280,1280]{1,0:T(8,128)(2,1)} %weight_hbm.1, ...), custom_call_target="tpu_custom_call" | custom-call | tf_op jit(solution)/shard_map/pallas_call | solution.py:496
  58.5 3.3 %copy.12 = bf16[2,32,2,5120]{3,2,1,0:T(2,128)(2,1)} copy(bf16[2,32,2,5120]{3,2,1,0:T(2,128)(2,1)} %shard_map.100) | data formatting | bytes 2621440
